TPU v7x, 32 devices: a whole 2x2x4 slice. The times are simulated.
32 devices in a mesh: groups: 1, tensor: 16 (over z, y, x), sub: 2 (over core).
Axes of the slice: x: 2, y: 2, z: 4, core: 2. Of those that a mesh axis runs over, the one named last changes fastest.
Arguments:
- stored: bfloat16 [8192, 32768], P(('tensor', 'sub')), may hold values from -0.0625 to 0.0625
- tokens: bfloat16 [256, 8192], P(('groups', 'tensor')), may hold values from -6 to 6
- owner_map: int32 [256], replicated, may hold values from 0 to 255, each once
- live_count: int32 [1], P('groups'), may hold values from 128 to 256
Outputs:
- serving_out: bfloat16 [256, 32768], P('groups', ('tensor', 'sub'))
Inputs may be any that keep to these rules, and one draw needn't show every extreme that they name: `owner_map`: each of the 256 saved column blocks is named exactly once. Rows from live_count on are padding.
All inputs are finite; a program needn't handle non-finite values.
Results may differ from a plain program's by a relative error of at most 0.001.
Values may be sent and summed in bfloat16 or wider, within the bound.
A program may use at most 128 MiB of HBM per device.

v0:
```python
import jax
import jax.numpy as jnp
from jax import lax
from jax.sharding import PartitionSpec as P


def on_device(stored, tokens, owner_map, live_count):
    row_count = stored.shape[0]
    block_count = owner_map.shape[0]
    width = stored.shape[1] // block_count
    devices = lax.axis_size(("tensor", "sub"))
    per_dev = block_count // devices
    ordered = jnp.take(stored.reshape(row_count, block_count, width), owner_map, axis=1)
    gathered = lax.all_gather(tokens, "tensor", axis=0, tiled=True)
    sectioned = ordered.reshape(row_count, devices, per_dev, width)
    piece = lax.all_to_all(sectioned, ("tensor", "sub"), split_axis=1, concat_axis=0, tiled=True)
    weights = piece.reshape(piece.shape[0], piece.shape[2], piece.shape[3])
    result = jnp.einsum("td,dkc->tkc", gathered, weights, preferred_element_type=jnp.float32)
    product = result.reshape(result.shape[0], per_dev * width)
    row_ids = lax.broadcasted_iota(jnp.int32, (product.shape[0], 1), 0)
    keep = row_ids < live_count[0]
    return jnp.where(keep, product, jnp.float32(0.0)).astype(jnp.bfloat16)


def solution(mesh):
    placed = (P(("tensor", "sub"), None), P(("groups", "tensor"), None), P(), P("groups"))
    return jax.shard_map(
        on_device,
        mesh=mesh,
        in_specs=placed,
        out_specs=P("groups", ("tensor", "sub")),
        check_vma=False,
    )
```

profile of v0, /device:TPU:0, one launch (start us, length us, event | category | flops | bytes accessed | tf_op | source)
XLA Modules:
  0.0 526.8 jit_solution(14248439712817356019)
XLA Ops:
  6.5 0.7 compare_select_fusion
  7.2 0.7 compare_and_fusion
  7.9 22.3 %copy.14 = bf16[256,32768]{0,1:T(8,128)(2,1)} copy(bf16[256,32768]{1,0:T(8,128)(2,1)} %param.4) | data formatting | bytes 33554432 | tf_op args[0]
  30.3 22.4 %copy.15 = bf16[256,256,128]{2,0,1:T(8,128)(2,1)} copy(bf16[256,256,128]{0,2,1:T(8,128)(2,1)} %bitcast.18) | data formatting | bytes 33554432 | tf_op jit(solution)/shard_map/reshape | solution.py:13
  52.6 0.1 broadcast_in_dim.27
  52.7 15.5 %gather_fusion = bf16[256,256,128]{2,1,0:T(8,128)(2,1)} fusion(bf16[256,256,128]{2,0,1:T(8,128)(2,1)} %copy.15, s32[1024]{0:T(1024)S(1)} %pad_clamp_fusion), kind=kCustom, calls=%fused_computation | custom fusion | bytes 33555456 | tf_op jit(solution)/shard_map/jit(_take)/gather | solution.py:13
  68.3 14.9 %bitcast_select_fusion = bf16[256,32,8,128]{3,2,1,0:T(8,128)(2,1)S(1)} fusion(bf16[256,256,128]{2,0,1:T(8,128)(2,1)} %bitcast.17, pred[32,8]{1,0:T(8,128)(4,1)S(1)} %broadcast_in_dim.27), kind=kLoop, calls=%fused_computation.3 | loop fusion | flops 8388608 | bytes 33554688 | tf_op jit(solution)/shard_map/jit(_take)/select_n | solution.py:13
  83.1 7.4 %copy.17 = bf16[256,32,8,128]{3,2,0,1:T(8,128)(2,1)} copy(bf16[256,32,8,128]{3,2,1,0:T(8,128)(2,1)S(1)} %bitcast_select_fusion) | data formatting | bytes 33554432 | tf_op jit(solution)/shard_map/jit(_take)/select_n | solution.py:13
  90.5 7.5 %all-to-all-start = ((bf16[256,32,8,128]{3,2,0,1:T(8,128)(2,1)}), bf16[256,32,8,128]{3,2,0,1:T(8,128)(2,1)}, u32[]{:S(2)}, u32[]{:S(2)}) async-start(bf16[256,32,8,128]{3,2,0,1:T(8,128)(2,1)} %copy.17), calls=%async_computation | async-start | bytes 33554432 | tf_op jit(solution)/shard_map/all_to_all | solution.py:16
  98.0 0.0 all-gather.2.cloned.1.call-start
  98.0 0.7 all-gather.2.cloned.1.call-update
  99.4 207.7 %all-gather.2.cloned.1.call-done = bf16[256,8192]{1,0:T(8,128)(2,1)} async-done(((bf16[16,8192]{1,0:T(8,128)(2,1)}), bf16[256,8192]{1,0:T(8,128)(2,1)}) %all-gather.2.cloned.1.call-update) | async-done | bytes 4194320 | tf_op jit(solution)/shard_map/all_gather | solution.py:14
  307.0 200.0 %all-to-all-done = bf16[256,32,8,128]{3,2,0,1:T(8,128)(2,1)} async-done(((bf16[256,32,8,128]{3,2,0,1:T(8,128)(2,1)}), bf16[256,32,8,128]{3,2,0,1:T(8,128)(2,1)}, u32[]{:S(2)}, u32[]{:S(2)}) %all-to-all-start) | async-done | bytes 16777248 | tf_op jit(solution)/shard_map/all_to_all | solution.py:16
  507.1 11.7 %fusion = bf16[8,128,256]{2,1,0:T(8,128)(2,1)S(1)} fusion(bf16[8192,8,128]{2,1,0:T(8,128)(2,1)} %bitcast.6, bf16[256,8192]{1,0:T(8,128)(2,1)} %all-gather.2.cloned.1.call-done), kind=kOutput, calls=%fused_computation.1 | convolution fusion | flops 4294967296 | bytes 21495808 | tf_op jit(solution)/shard_map/td,dkc->tkc/dot_general | solution.py:18
  518.8 0.2 copy.19
  519.0 1.0 select_convert_fusion
  (2 shorter events, 0.0 us)
Async XLA Ops:
  90.5 416.5 %all-to-all-start = ((bf16[256,32,8,128]{3,2,0,1:T(8,128)(2,1)}), bf16[256,32,8,128]{3,2,0,1:T(8,128)(2,1)}, u32[]{:S(2)}, u32[]{:S(2)}) async-start(bf16[256,32,8,128]{3,2,0,1:T(8,128)(2,1)} %copy.17), calls=%async_computation | async-start | bytes 33554432 | tf_op jit(solution)/shard_map/all_to_all | solution.py:16
  98.0 209.1 %all-gather.2.cloned.1.call-start = ((), (), s32[]{:S(2)}) async-start(), calls=%async_computation.1 | async-start | bytes 4456448 | tf_op jit(solution)/shard_map/all_gather | solution.py:14
Sparse Core Ops, SparseCore 0:
  101.6 205.4 all-gather.1
where the time goes:
time: 528 us; the launch traced here: 527 us
  waiting for transfers between devices  408 us (77%)
  local copies, waits for them, and re-layouts  67.9 us (13%)
  other arithmetic  17.2 us (3%)
  between operations  14.1 us (3%)
  matrix products  11.7 us (2%)
  starting transfers between devices  7.5 us (1%)
    all_gather x1, waiting for transfers between devices, on_device(): gathered = lax.all_gather(tokens, 'tensor', axis=0, tiled=True)  208 us
    all_to_all x1, waiting for transfers between devices, on_device(): lax.all_to_all(sectioned, ('tensor', 'sub'), split_axis=1, concat_axis=0,...  200 us
    reshape x1, local copies, waits for them, and re-layouts, on_device(): stored.reshape(row_count, block_count, width)  22.4 us
    unnamed x1, local copies, waits for them, and re-layouts  22.3 us
    select_n x2, other arithmetic, on_device(): jnp.take(stored.reshape(row_count, block_count, width), owner_map, axis=1)  15.5 us
    gather x1, local copies, waits for them, and re-layouts, on_device(): jnp.take(stored.reshape(row_count, block_count, width), owner_map, axis=1)  15.5 us
    dot_general x1, matrix products, on_device(): jnp.einsum('td,dkc->tkc', gathered, weights, preferred_element_type=jnp.f...  11.7 us
  transfers between devices with their start and end apart: 2, of which 2 were waited for; matrix products, arithmetic and copies ran while one was open for 0% of the time, Pallas kernels for 0%

commit v1 on v0

--- a/solution.py
+++ b/solution.py
@@ -1,10 +1,17 @@
+import functools
+
 import jax
 import jax.numpy as jnp
 from jax import lax
+from jax.experimental import pallas as pl
+from jax.experimental.pallas import tpu as pltpu
 from jax.sharding import PartitionSpec as P
 
-
-def on_device(stored, tokens, owner_map, live_count):
+MESH = pl.DeviceIdType.MESH
+VMEM_LIMIT = 67043328
+
+
+def portable(stored, tokens, owner_map, live_count):
     row_count = stored.shape[0]
     block_count = owner_map.shape[0]
     width = stored.shape[1] // block_count
@@ -22,6 +29,203 @@
     return jnp.where(keep, product, jnp.float32(0.0)).astype(jnp.bfloat16)
 
 
+def kernel(T, Z, own_rows, block, half, map_ref, tok_ref, w_hbm, out_ref,
+           w, tok, stage, wr, p, r1, r2, rz,
+           w_sem, ts, tr, ss, sr, s1s, s1r, s2s, s2r, zs, zr):
+    t = lax.axis_index("tensor")
+    s = lax.axis_index("sub")
+    x, y, z = lax.rem(t, 2), lax.rem(t // 2, 2), t // 4
+    depth = w.shape[1]
+    other = 1 - s
+    x_far = t + 1 - 2 * x
+    y_far = t + 2 - 4 * y
+    firsts = 4 * Z
+
+    def load_block(b, carry):
+        at = pl.multiple_of(b * block, block)
+        pltpu.make_async_copy(w_hbm.at[:, pl.ds(at, block)], w.at[b], w_sem).start()
+        return carry
+
+    lax.fori_loop(0, w.shape[0], load_block, 0)
+
+    barrier = pltpu.get_barrier_semaphore()
+    for r in range(1, T):
+        pl.semaphore_signal(barrier, inc=1, device_id={"tensor": lax.rem(t + r, T), "sub": s}, device_id_type=MESH)
+    pl.semaphore_signal(barrier, inc=1, device_id={"tensor": t, "sub": other}, device_id_type=MESH)
+    pl.semaphore_wait(barrier, T)
+
+    def token_copy(r):
+        to = lax.rem(t + r, T)
+        return pltpu.make_async_remote_copy(
+            src_ref=tok_ref.at[:, pl.ds(pl.multiple_of(to * 2 * depth, 2 * depth), 2 * depth)],
+            dst_ref=tok.at[pl.ds(pl.multiple_of(t * own_rows, own_rows), own_rows), :],
+            send_sem=ts.at[r], recv_sem=tr.at[r],
+            device_id={"tensor": to, "sub": s}, device_id_type=MESH)
+
+    for r in range(1, T):
+        token_copy(r).start()
+    tok[pl.ds(pl.multiple_of(t * own_rows, own_rows), own_rows), :] = (
+        tok_ref[:, pl.ds(pl.multiple_of(t * 2 * depth, 2 * depth), 2 * depth)])
+
+    def sub_copy(h, j):
+        return pltpu.make_async_remote_copy(
+            src_ref=stage.at[j], dst_ref=wr.at[4 * h + j],
+            send_sem=ss.at[j], recv_sem=sr.at[4 * h + j],
+            device_id={"tensor": t, "sub": other}, device_id_type=MESH)
+
+    def first_copy(g, j):
+        return pltpu.make_async_remote_copy(
+            src_ref=p.at[4 * g + j], dst_ref=r1.at[4 * g + j],
+            send_sem=s1s.at[4 * g + j], recv_sem=s1r.at[4 * g + j],
+            device_id={"tensor": y_far if j % 2 else x_far, "sub": s}, device_id_type=MESH)
+
+    def second_copy(g, j):
+        return pltpu.make_async_remote_copy(
+            src_ref=p.at[firsts + 4 * g + j], dst_ref=r2.at[2 * g + j],
+            send_sem=s2s.at[2 * g + j], recv_sem=s2r.at[2 * g + j],
+            device_id={"tensor": x_far if j % 2 else y_far, "sub": s}, device_id_type=MESH)
+
+    def z_copy(g, j):
+        to = lax.rem(t + 4 * (g + 1), T)
+        return pltpu.make_async_remote_copy(
+            src_ref=p.at[firsts + 4 * g + 2 + j], dst_ref=rz.at[2 * g + j],
+            send_sem=zs.at[2 * g + j], recv_sem=zr.at[2 * g + j],
+            device_id={"tensor": to, "sub": s}, device_id_type=MESH)
+
+    def first_block(h, j, sub):
+        kept, g = h // Z, lax.rem(h, Z)
+        rx = (1 - kept, 1, 1 - kept, 0)[j]
+        ry = (1, 1 - kept, 0, 1 - kept)[j]
+        to = lax.rem(z + g + 1, Z) * 4 + lax.rem(y + ry, 2) * 2 + lax.rem(x + rx, 2)
+        return (2 * to + sub) * (2 * half) + (j % 2) * half
+
+    def columns(base, m):
+        return w[map_ref[base + m]]
+
+    def fill(h, j):
+        base = first_block(h, j, other)
+        for m in range(half):
+            stage[j, :, m * block:(m + 1) * block] = columns(base, m)
+        sub_copy(h, j).start()
+
+    pltpu.make_async_copy(w, w, w_sem).wait()
+    for j in range(4):
+        fill(0, j)
+    for r in range(1, T):
+        token_copy(r).wait()
+
+    rows = p.shape[1]
+
+    def body(h, carry):
+        mine = tok[0:rows, pl.ds(pl.multiple_of(s * depth, depth), depth)]
+        theirs = tok[0:rows, pl.ds(pl.multiple_of(other * depth, depth), depth)]
+        for j in range(4):
+            base = first_block(h, j, s)
+            own = jnp.concatenate([columns(base, m) for m in range(half)], axis=1)
+            total = jnp.dot(mine, own, preferred_element_type=jnp.float32)
+            sub_copy(h, j).wait()
+            total += jnp.dot(theirs, wr[4 * h + j], preferred_element_type=jnp.float32)
+            p[4 * h + j] = total
+
+            @pl.when(h < 2)
+            def _():
+                first_copy(h, j).start()
+
+            @pl.when(h < 2 * Z - 1)
+            def _():
+                fill(h + 1, j)
+        return carry
+
+    lax.fori_loop(0, 2 * Z, body, 0)
+
+    def second(g):
+        for j in range(2):
+            second_copy(g, j).wait_recv()
+            p[firsts + 4 * g + 2 + j] += r2[2 * g + j]
+            if g < Z - 1:
+                z_copy(g, j).start()
+
+    for g in range(Z):
+        for j in range(2):
+            first_copy(g, j).wait_recv()
+            p[firsts + 4 * g + j] += r1[4 * g + j]
+            second_copy(g, j).start()
+        if g + 2 < Z:
+            for j in range(4):
+                first_copy(g + 2, j).start()
+        for j in range(2, 4):
+            first_copy(g, j).wait_recv()
+            p[firsts + 4 * g + j] += r1[4 * g + j]
+        if g >= 1:
+            second(g - 1)
+    second(Z - 1)
+    wide = half * block
+    for j in range(2):
+        total = p[firsts + 4 * (Z - 1) + 2 + j]
+        for g in range(Z - 1):
+            z_copy(g, j).wait_recv()
+            total += rz[2 * g + j]
+        out_ref[0:rows, j * wide:(j + 1) * wide] = total.astype(out_ref.dtype)
+    for g in range(Z):
+        for j in range(4):
+            first_copy(g, j).wait_send()
+        for j in range(2):
+            second_copy(g, j).wait_send()
+            if g < Z - 1:
+                z_copy(g, j).wait_send()
+
+
+def plan(depth, ff, own_rows, block, T, n_blocks):
+    Z = T // 4
+    wide = ff // (4 * T)
+    rows = own_rows * T
+    sems = pltpu.SemaphoreType.DMA
+    f32, bf16 = jnp.float32, jnp.bfloat16
+    return [
+        pltpu.VMEM((n_blocks, depth, block), bf16),
+        pltpu.VMEM((rows, 2 * depth), bf16),
+        pltpu.VMEM((4, depth, wide), bf16),
+        pltpu.VMEM((8 * Z, depth, wide), bf16),
+        pltpu.VMEM((8 * Z, rows, wide), f32),
+        pltpu.VMEM((4 * Z, rows, wide), f32),
+        pltpu.VMEM((2 * Z, rows, wide), f32),
+        pltpu.VMEM((2 * Z, rows, wide), f32),
+    ] + [sems(()), sems((T,)), sems((T,)), sems((4,)), sems((8 * Z,)), sems((4 * Z,)), sems((4 * Z,)),
+         sems((2 * Z,)), sems((2 * Z,)), sems((2 * Z,)), sems((2 * Z,))]
+
+
+def fits(depth, ff, own_rows, block, T, subs, n_blocks):
+    if T % 4 or T < 8 or subs != 2 or n_blocks % (4 * T):
+        return False
+    rows, wide, Z = own_rows * T, ff // (4 * T), T // 4
+    used = 2 * (depth * ff + rows * 2 * depth + (4 + 8 * Z) * depth * wide) + 4 * (16 * Z * rows * wide)
+    return used + (4 << 20) < VMEM_LIMIT
+
+
+def on_device(stored, tokens, owner_map, live_count):
+    depth, ff = stored.shape
+    own_rows = tokens.shape[0]
+    n_blocks = owner_map.shape[0]
+    block = ff // n_blocks
+    T, subs = lax.axis_size("tensor"), lax.axis_size("sub")
+    if not fits(depth, ff, own_rows, block, T, subs, n_blocks):
+        return portable(stored, tokens, owner_map, live_count)
+    rows = own_rows * T
+    half = n_blocks // (4 * T)
+    product = pl.pallas_call(
+        functools.partial(kernel, T, T // 4, own_rows, block, half),
+        out_shape=jax.ShapeDtypeStruct((rows, ff // (2 * T)), jnp.bfloat16),
+        in_specs=[pl.BlockSpec(memory_space=pltpu.SMEM), pl.BlockSpec(memory_space=pltpu.VMEM),
+                  pl.BlockSpec(memory_space=pl.ANY)],
+        out_specs=pl.BlockSpec(memory_space=pltpu.VMEM),
+        scratch_shapes=plan(depth, ff, own_rows, block, T, n_blocks),
+        compiler_params=pltpu.CompilerParams(
+            collective_id=0, has_side_effects=True, vmem_limit_bytes=VMEM_LIMIT),
+    )(owner_map, tokens, stored)
+    keep = lax.broadcasted_iota(jnp.int32, (rows, 1), 0) < live_count[0]
+    return jnp.where(keep, product, jnp.bfloat16(0.0))
+
+
 def solution(mesh):
     placed = (P(("tensor", "sub"), None), P(("groups", "tensor"), None), P(), P("groups"))
     return jax.shard_map(

time: 528 us -> 180 us (0.34)
  waiting for transfers between devices: 408 us -> 0 us
  Pallas kernels: 0 us -> 177 us
  local copies, waits for them, and re-layouts: 67.9 us -> 0 us
  other arithmetic: 17.2 us -> 2.54 us
  between operations: 14.1 us -> 0.66 us
  matrix products: 11.7 us -> 0 us
  starting transfers between devices: 7.5 us -> 0 us
    all_gather x1 -> x0, waiting for transfers between devices: 208 us -> none  [on_device(): gathered = lax.all_gather(tokens, 'tensor', axis=0, tiled=True)]
    all_to_all x1 -> x0, waiting for transfers between devices: 200 us -> none  [on_device(): lax.all_to_all(sectioned, ('tensor', 'sub'), split_axis=1, concat_axis=0,...]
    pallas_call x0 -> x1, Pallas kernels: none -> 177 us  [on_device(): pl.pallas_call(functools.partial(kernel, T, T // 4, own_rows, block, half...]
    reshape x2 -> x0, local copies, waits for them, and re-layouts: 22.6 us -> none  [the longest x1 22.4 us: on_device(): stored.reshape(row_count, block_count, width)]
    unnamed x1 -> x0, local copies, waits for them, and re-layouts: 22.3 us -> none
    gather x1 -> x0, local copies, waits for them, and re-layouts: 15.5 us -> none  [on_device(): jnp.take(stored.reshape(row_count, block_count, width), owner_map, axis=1)]
    select_n x2 -> x1, other arithmetic: 15.5 us -> 1.95 us  [on_device(): return jnp.where(keep, product, jnp.bfloat16(0.0))]
    dot_general x1 -> x0, matrix products: 11.7 us -> none  [on_device(): jnp.einsum('td,dkc->tkc', gathered, weights, preferred_element_type=jnp.f...]
  transfers between devices with their start and end apart: 2 -> 0, of which waited for: 2 -> 0; matrix products, arithmetic and copies ran while one was open for 0% -> 0% of each run, Pallas kernels for 0% -> 0%
where the time goes in v1:
time: 180 us
  Pallas kernels  177 us (98%)
  other arithmetic  2.54 us (1%)
    pallas_call x1, Pallas kernels, on_device(): pl.pallas_call(functools.partial(kernel, T, T // 4, own_rows, block, half...  177 us

profile of v1, /device:TPU:0, one launch (start us, length us, event | category | flops | bytes accessed | tf_op | source)
XLA Modules:
  0.0 179.8 jit_solution(5085254953034250705)
XLA Ops:
  0.7 0.6 iota_compare_fusion
  1.3 176.6 %shard_map.46 = bf16[256,1024]{1,0:T(8,128)(2,1)} custom-call(s32[256]{0:T(256)} %map_ref.1, bf16[16,8192]{1,0:T(8,128)(2,1)} %tok_ref.1, bf16[256,32768]{1,0:T(8,128)(2,1)} %w_hbm.1), custom_call_target="tpu_custom_call" | custom-call | tf_op jit(solution)/shard_map/pallas_call | solution.py:215
  177.8 1.9 %broadcast_select_fusion = bf16[256,1024]{1,0:T(8,128)(2,1)} fusion(bf16[256,1024]{1,0:T(8,128)(2,1)} %shard_map.46, pred[256]{0:T(512)(128)(4,1)} %iota_compare_fusion), kind=kLoop, calls=%fused_computation | loop fusion | flops 262144 | bytes 1048832 | tf_op jit(solution)/shard_map/jit(_where)/select_n | solution.py:226
